TPU v7x, 32 devices: a whole 2x2x4 slice. The times are simulated.
32 devices in a mesh: grp: 2 (over y), ctx: 4 (over z), tp: 2 (over x), sub: 2 (over core).
Axes of the slice: x: 2, y: 2, z: 4, core: 2. Of those that a mesh axis runs over, the one named last changes fastest.
Arguments:
- context: bfloat16 [3072, 2048], P(('grp', 'ctx'), ('tp', 'sub')), parts along dimension 0, may hold values from -24 to 24
- context_pos: int32 [3072], P(('grp', 'ctx')), parts along dimension 0, may hold values from 0 to 1535, each once
- latent_in: bfloat16 [64, 2048], P(('grp', 'ctx')), parts along dimension 0, may hold values from -24 to 24
- latent_start: int32 [2], P('grp'), parts along dimension 0, may hold values from 768 to 1504
- ctx_gain: float32 [2048], replicated, may hold values from 0.25 to 1.75
- lat_gain: float32 [2048], replicated, may hold values from 0.25 to 1.75
- mid_gain: float32 [2048], replicated, may hold values from 0.25 to 1.75
- cross_q: bfloat16 [2048, 2048], P('ctx', ('tp', 'sub')), may hold values from -2 to 2
- cross_k: bfloat16 [2048, 2048], P('ctx', ('tp', 'sub')), may hold values from -2 to 2
- cross_v: bfloat16 [2048, 2048], P('ctx', ('tp', 'sub')), may hold values from -0.125 to 0.125
- cross_out: bfloat16 [2048, 2048], P('ctx', ('tp', 'sub')), may hold values from -0.125 to 0.125
- self_qkv: bfloat16 [2048, 3, 2048], P('ctx', None, ('tp', 'sub')), may hold values from -2 to 2
- self_out: bfloat16 [2048, 2048], P('ctx', ('tp', 'sub')), may hold values from -0.125 to 0.125
Outputs:
- latent_out: bfloat16 [64, 2048], P(('grp', 'ctx'), ('tp', 'sub')), parts along dimension 0
There are 2 independent parts, one for each index of `grp`. A program takes and returns all parts, laid end to end along the dimension named above; an argument that names none is the same for every part. Nothing has to cross between parts.
Inputs may be any that keep to these rules, and one draw needn't show every extreme that they name: context_pos holds each of 0 to 1535 once.
All inputs are finite; a program needn't handle non-finite values.
Results may differ from a plain program's by a relative error of at most 0.035.
Values may be sent and summed in bfloat16 or wider, within the bound.
A program may use at most 64 MiB of HBM per device.

v0:
```python
import math
import jax
import jax.numpy as jnp
from jax import lax
from jax.sharding import PartitionSpec as P

DH = 128
EPS = 1e-05
NEG = -1e30
HEADS_AXES = ("tp", "sub")


def contract_last(left, right):
    return lax.dot_general(
        left, right, (((1,), (1,)), ((), ())), preferred_element_type=jnp.float32
    )


def summed_over(partial, axis):
    everything = lax.all_gather(partial.astype(jnp.bfloat16), axis)
    return jnp.sum(everything.astype(jnp.float32), axis=0)


def on_device(
    context,
    context_pos,
    latent_in,
    latent_start,
    ctx_gain,
    lat_gain,
    mid_gain,
    cross_q,
    cross_k,
    cross_v,
    cross_out,
    self_qkv,
    self_out,
):
    rows, width = latent_in.shape
    depth, columns = cross_q.shape
    shards = lax.axis_size("ctx")
    heads = columns // DH
    latents = rows * shards
    own = lax.axis_index("ctx")
    mine = lambda array: lax.dynamic_slice_in_dim(array, own * depth, depth, array.ndim - 1)
    whole = lax.all_gather(context, HEADS_AXES, axis=1, tiled=True)
    all_latents = lax.all_gather(latent_in, "ctx", axis=0, tiled=True).astype(jnp.float32)
    lat_scale = lax.rsqrt(jnp.mean(all_latents * all_latents, axis=1, keepdims=True) + EPS)
    lat_part = mine(all_latents)
    normed_lat = (lat_part * lat_scale * mine(lat_gain)).astype(jnp.bfloat16)
    queries = summed_over(
        jnp.dot(normed_lat, cross_q, preferred_element_type=jnp.float32), "ctx"
    ).astype(jnp.bfloat16)
    split = [slice(head * DH, head * DH + DH) for head in range(heads)]
    absorbed = jnp.concatenate(
        [contract_last(queries[:, cut], cross_k[:, cut]) for cut in split], axis=0
    )
    absorbed = (absorbed * (mine(ctx_gain) * (1.0 / math.sqrt(DH)))).astype(jnp.bfloat16)
    absorbed = lax.all_gather(absorbed, "ctx", axis=1, tiled=True)
    wide = whole.astype(jnp.float32)
    token_scale = lax.rsqrt(jnp.mean(wide * wide, axis=1) + EPS)
    scores = contract_last(absorbed, whole) * token_scale[None, :]
    query_pos = latent_start[0] + jnp.arange(latents, dtype=jnp.int32)
    allowed = jnp.tile(context_pos[None, :] <= query_pos[:, None], (heads, 1))
    scores = jnp.where(allowed, scores, NEG)
    top = jnp.max(scores, axis=1, keepdims=True)
    weights = jnp.where(allowed, jnp.exp(scores - top), 0.0)
    total = jnp.sum(weights, axis=1, keepdims=True)
    mixed = jnp.dot(
        (weights * token_scale[None, :]).astype(jnp.bfloat16),
        whole,
        preferred_element_type=jnp.float32,
    ).astype(jnp.bfloat16)
    mixed = lax.all_to_all(
        mixed.reshape(heads * latents, shards, depth), "ctx", split_axis=1, concat_axis=0
    ).reshape(shards, heads * latents, depth)
    stats = lax.all_gather(jnp.concatenate([top, total], axis=1), "ctx")
    tops, totals = (stats[:, :, :1], stats[:, :, 1:])
    factors = jnp.exp(tops - jnp.max(tops, axis=0))
    mixed = jnp.sum(mixed.astype(jnp.float32) * factors, axis=0) / jnp.sum(totals * factors, axis=0)
    mixed = (mixed * mine(ctx_gain)).astype(jnp.bfloat16)
    attended = jnp.concatenate(
        [
            jnp.dot(
                mixed[head * latents : (head + 1) * latents],
                cross_v[:, cut],
                preferred_element_type=jnp.float32,
            )
            for head, cut in enumerate(split)
        ],
        axis=1,
    )
    attended = summed_over(attended, "ctx").astype(jnp.bfloat16)
    cross_sum = summed_over(contract_last(attended, cross_out), HEADS_AXES)
    hidden = (lat_part + cross_sum).astype(jnp.bfloat16).astype(jnp.float32)
    squares = jnp.sum(lax.all_gather(jnp.sum(hidden * hidden, axis=1), "ctx"), axis=0)
    hidden_scale = lax.rsqrt(squares / width + EPS)
    projected = jnp.dot(
        (hidden * mine(mid_gain)).astype(jnp.bfloat16),
        self_qkv.reshape(depth, 3 * columns),
        preferred_element_type=jnp.float32,
    )
    projected = summed_over(projected, "ctx") * hidden_scale[:, None]
    projected = projected.astype(jnp.bfloat16).reshape(latents, 3, columns)
    index = jnp.arange(latents, dtype=jnp.int32)
    causal = index[None, :] <= index[:, None]
    parts = []
    for cut in split:
        scores = contract_last(projected[:, 0, cut], projected[:, 1, cut]) * (1.0 / math.sqrt(DH))
        scores = jnp.where(causal, scores, NEG)
        weights = jnp.where(causal, jnp.exp(scores - jnp.max(scores, axis=1, keepdims=True)), 0.0)
        numerator = jnp.dot(
            weights.astype(jnp.bfloat16), projected[:, 2, cut], preferred_element_type=jnp.float32
        )
        parts.append(numerator / jnp.sum(weights, axis=1, keepdims=True))
    attended_self = jnp.concatenate(parts, axis=1).astype(jnp.bfloat16)
    self_sum = summed_over(contract_last(attended_self, self_out), HEADS_AXES)
    result = (hidden + self_sum).astype(jnp.bfloat16)
    result = lax.all_to_all(
        result.reshape(shards, rows, depth), "ctx", split_axis=0, concat_axis=1
    ).reshape(rows, width)
    return lax.dynamic_slice_in_dim(result, lax.axis_index(HEADS_AXES) * columns, columns, 1)


def solution(mesh):
    return jax.shard_map(
        on_device,
        mesh=mesh,
        in_specs=(
            P(("grp", "ctx"), ("tp", "sub")),
            P(("grp", "ctx")),
            P(("grp", "ctx"), None),
            P("grp"),
            P(),
            P(),
            P(),
            P("ctx", ("tp", "sub")),
            P("ctx", ("tp", "sub")),
            P("ctx", ("tp", "sub")),
            P("ctx", ("tp", "sub")),
            P("ctx", None, ("tp", "sub")),
            P("ctx", ("tp", "sub")),
        ),
        out_specs=P(("grp", "ctx"), ("tp", "sub")),
        check_vma=False,
    )
```

profile of v0, /device:TPU:0, one launch (start us, length us, event | category | flops | bytes accessed | tf_op | source)
XLA Modules:
  0.0 152.7 jit_solution(14311558146944119064)
XLA Ops:
  6.5 0.7 all-gather.8.cloned.1.call-update
  7.3 15.3 %all_gather.49 = bf16[32,2048]{1,0:T(8,128)(2,1)S(1)} all-gather(bf16[8,2048]{1,0:T(8,128)(2,1)} %param.15), channel_id=1, replica_groups=mesh['grp'=2,'ctx'=4,'tp'=2,'sub'=2] {'ctx'}, dimensions={0}, use_global_device_ids=true | all-gather | bytes 163840 | tf_op jit(solution)/shard_map/all_gather | solution.py:47
  23.4 0.8 dynamic_slice.17
  24.4 13.7 %all-gather = bf16[128,512]{1,0:T(8,128)(2,1)S(1)} all-gather(bf16[32,512]{1,0:T(8,128)(2,1)S(1)} %convolution_convert_fusion.4), channel_id=2, replica_groups=mesh['grp'=2,'ctx'=4,'tp'=2,'sub'=2] {'ctx'}, dimensions={0}, use_global_device_ids=true | all-gather | bytes 163840 | tf_op jit(solution)/shard_map/all_gather | solution.py:20
  38.1 0.8 broadcast_multiply_fusion
  39.5 15.5 %all_gather.52 = bf16[128,2048]{1,0:T(8,128)(2,1)S(1)} all-gather(bf16[128,512]{1,0:T(8,128)(2,1)S(1)} %fusion.14), channel_id=1, replica_groups=mesh['grp'=2,'ctx'=4,'tp'=2,'sub'=2] {'ctx'}, dimensions={1}, use_global_device_ids=true | all-gather | bytes 655360 | tf_op jit(solution)/shard_map/all_gather | solution.py:59
  55.1 1.9 %multiply_reduce_fusion = f32[384]{0:T(512)S(1)} fusion(bf16[384,2048]{1,0:T(8,128)(2,1)} %all-gather.8.cloned.1.call-done), kind=kLoop, calls=%fused_computation | loop fusion | flops 2358912 | bytes 1574400 | tf_op jit(solution)/shard_map/reduce_sum | solution.py:61
  57.1 0.7 fusion.104
  58.8 0.9 copy.17
  59.7 4.7 %all-to-all-start = ((bf16[1,128,4,512]{3,1,0,2:T(8,128)(2,1)}), bf16[1,128,4,512]{3,1,0,2:T(8,128)(2,1)S(1)}, u32[]{:S(2)}, u32[]{:S(2)}) async-start(bf16[1,128,4,512]{3,1,0,2:T(8,128)(2,1)} %copy.17), calls=%async_computation | async-start | bytes 1048576 | tf_op jit(solution)/shard_map/all_to_all | solution.py:74
  64.4 0.8 dynamic_slice.19
  65.2 1.7 %copy.18 = bf16[512,3,512]{0,2,1:T(8,128)(2,1)S(1)} copy(bf16[512,3,512]{2,0,1:T(8,128)(2,1)} %param.24) | data formatting | bytes 3145728 | tf_op args[11]
  68.2 11.4 %all-gather.1 = f32[512,2]{0,1:T(2,128)S(1)} all-gather(f32[128,2]{0,1:T(2,128)S(1)} %pad_maximum_fusion.1), channel_id=3, replica_groups=mesh['grp'=2,'ctx'=4,'tp'=2,'sub'=2] {'ctx'}, dimensions={0}, use_global_device_ids=true | all-gather | bytes 5120 | tf_op jit(solution)/shard_map/all_gather | solution.py:77
  80.0 1.0 fusion.10
  81.0 1.0 fusion.11
  82.0 1.0 fusion.12
  83.1 1.0 fusion.9
  84.2 13.4 %all_gather.56 = bf16[4,32,512]{2,1,0:T(8,128)(2,1)S(1)} all-gather(bf16[1,32,512]{2,1,0:T(8,128)(2,1)S(1)} %pad_maximum_fusion), channel_id=1, replica_groups=mesh['grp'=2,'ctx'=4,'tp'=2,'sub'=2] {'ctx'}, dimensions={0}, use_global_device_ids=true | all-gather | bytes 163840 | tf_op jit(solution)/shard_map/all_gather | solution.py:20
  97.8 5.4 %all-gather.2 = bf16[128,512]{1,0:T(8,128)(2,1)S(1)} all-gather(bf16[32,512]{1,0:T(8,128)(2,1)S(1)} %convolution_convert_fusion.3), channel_id=4, replica_groups=mesh['grp'=2,'ctx'=4,'tp'=2,'sub'=2] {'tp','sub'}, dimensions={0}, use_global_device_ids=true | all-gather | bytes 163840 | tf_op jit(solution)/shard_map/all_gather | solution.py:20
  104.0 15.4 %all-gather.3 = bf16[128,1536]{1,0:T(8,128)(2,1)S(1)} all-gather(bf16[32,1536]{1,0:T(8,128)(2,1)S(1)} %convolution_convert_fusion.1), channel_id=5, replica_groups=mesh['grp'=2,'ctx'=4,'tp'=2,'sub'=2] {'ctx'}, dimensions={0}, use_global_device_ids=true | all-gather | bytes 491520 | tf_op jit(solution)/shard_map/all_gather | solution.py:20
  119.8 8.3 %all-reduce = f32[128]{0:T(128)S(1)} all-reduce(f32[128]{0:T(128)S(1)} %dynamic-update-slice), channel_id=6, replica_groups=mesh['grp'=2,'ctx'=4,'tp'=2,'sub'=2] {'ctx'}, use_global_device_ids=true, to_apply=%add | all-reduce | flops 128 | bytes 1024
  130.3 5.4 %all-gather.5 = bf16[128,512]{1,0:T(8,128)(2,1)S(1)} all-gather(bf16[32,512]{1,0:T(8,128)(2,1)S(1)} %convolution_convert_fusion.2), channel_id=7, replica_groups=mesh['grp'=2,'ctx'=4,'tp'=2,'sub'=2] {'tp','sub'}, dimensions={0}, use_global_device_ids=true | all-gather | bytes 163840 | tf_op jit(solution)/shard_map/all_gather | solution.py:20
  136.4 3.3 %all-to-all-start.1 = ((bf16[4,8,1,512]{3,1,2,0:T(8,128)(2,1)}), bf16[4,8,1,512]{3,1,2,0:T(8,128)(2,1)S(1)}, u32[]{:S(2)}, u32[]{:S(2)}) async-start(bf16[4,8,1,512]{3,1,2,0:T(8,128)(2,1)} %fusion.31), calls=%async_computation.1 | async-start | bytes 65536 | tf_op jit(solution)/shard_map/all_to_all | solution.py:119
  139.6 5.7 %all-to-all-done.1 = bf16[4,8,1,512]{3,1,2,0:T(8,128)(2,1)S(1)} async-done(((bf16[4,8,1,512]{3,1,2,0:T(8,128)(2,1)}), bf16[4,8,1,512]{3,1,2,0:T(8,128)(2,1)S(1)}, u32[]{:S(2)}, u32[]{:S(2)}) %all-to-all-start.1) | async-done | bytes 32800 | tf_op jit(solution)/shard_map/all_to_all | solution.py:119
  (72 shorter events, 7.9 us)
Async XLA Ops:
  6.5 17.6 %copy-start = (bf16[512,512]{1,0:T(8,128)(2,1)S(1)}, bf16[512,512]{1,0:T(8,128)(2,1)}, u32[]{:S(2)}) copy-start(bf16[512,512]{1,0:T(8,128)(2,1)} %param.20) | copy-start | bytes 1572868
  6.5 32.3 %copy-start.4 = (bf16[512,512]{1,0:T(8,128)(2,1)S(1)}, bf16[512,512]{1,0:T(8,128)(2,1)}, u32[]{:S(2)}) copy-start(bf16[512,512]{1,0:T(8,128)(2,1)} %param.21) | copy-start | bytes 1572868
  6.5 48.6 %all-gather.8.cloned.1.call-start = ((), (), s32[]{:S(2)}) async-start(), calls=%async_computation.2 | async-start | bytes 1966080 | tf_op jit(solution)/shard_map/all_gather | solution.py:46
  22.7 32.4 %copy-start.5 = (s32[384]{0:T(512)S(1)}, s32[384]{0:T(512)}, u32[]{:S(2)}) copy-start(s32[384]{0:T(512)} %param.14) | copy-start | bytes 4612
  55.1 2.0 %copy-start.1 = (bf16[384,2048]{1,0:T(8,128)(2,1)S(1)}, bf16[384,2048]{1,0:T(8,128)(2,1)}, u32[]{:S(2)}) copy-start(bf16[384,2048]{1,0:T(8,128)(2,1)} %all-gather.8.cloned.1.call-done) | copy-start | bytes 4718596
  59.7 20.0 %all-to-all-start = ((bf16[1,128,4,512]{3,1,0,2:T(8,128)(2,1)}), bf16[1,128,4,512]{3,1,0,2:T(8,128)(2,1)S(1)}, u32[]{:S(2)}, u32[]{:S(2)}) async-start(bf16[1,128,4,512]{3,1,0,2:T(8,128)(2,1)} %copy.17), calls=%async_computation | async-start | bytes 1048576 | tf_op jit(solution)/shard_map/all_to_all | solution.py:74
  65.2 1.8 %copy-start.6 = (u32[32]{0:T(128)S(1)}, u32[32]{0:T(128)}, u32[]{:S(2)}) copy-start(u32[32]{0:T(128)} %constant.45) | copy-start | bytes 388
  66.9 30.7 %copy-start.2 = (bf16[512,512]{1,0:T(8,128)(2,1)S(1)}, bf16[512,512]{1,0:T(8,128)(2,1)}, u32[]{:S(2)}) copy-start(bf16[512,512]{1,0:T(8,128)(2,1)} %param.23) | copy-start | bytes 1572868
  104.0 26.0 %copy-start.3 = (bf16[512,512]{1,0:T(8,128)(2,1)S(1)}, bf16[512,512]{1,0:T(8,128)(2,1)}, u32[]{:S(2)}) copy-start(bf16[512,512]{1,0:T(8,128)(2,1)} %param.25) | copy-start | bytes 1572868
  136.4 8.9 %all-to-all-start.1 = ((bf16[4,8,1,512]{3,1,2,0:T(8,128)(2,1)}), bf16[4,8,1,512]{3,1,2,0:T(8,128)(2,1)S(1)}, u32[]{:S(2)}, u32[]{:S(2)}) async-start(bf16[4,8,1,512]{3,1,2,0:T(8,128)(2,1)} %fusion.31), calls=%async_computation.1 | async-start | bytes 65536 | tf_op jit(solution)/shard_map/all_to_all | solution.py:119
Sparse Core Ops, SparseCore 0:
  8.9 22.3 all-gather.7
where the time goes:
time: 153 us
  blocking collectives  104 us (68%)
  between operations  14.9 us (10%)
  matrix products  8.52 us (6%)
  starting transfers between devices  8.01 us (5%)
  local copies, waits for them, and re-layouts  6.4 us (4%)
  waiting for transfers between devices  6.38 us (4%)
  other arithmetic  4.64 us (3%)
    all_gather x5, blocking collectives, summed_over(): everything = lax.all_gather(partial.astype(jnp.bfloat16), axis)  53.4 us
    all_gather x1, blocking collectives, on_device(): absorbed = lax.all_gather(absorbed, 'ctx', axis=1, tiled=True)  15.5 us
    all_gather x1, blocking collectives, on_device(): lax.all_gather(latent_in, 'ctx', axis=0, tiled=True).astype(jnp.float32)  15.3 us
    all_gather x1, blocking collectives, on_device(): stats = lax.all_gather(jnp.concatenate([top, total], axis=1), 'ctx')  11.4 us
    unnamed x1, blocking collectives  8.34 us
    all_to_all x1, waiting for transfers between devices, on_device(): lax.all_to_all(result.reshape(shards, rows, depth), 'ctx', split_axis=0,...  5.66 us
    all_to_all x1, starting transfers between devices, on_device(): lax.all_to_all(mixed.reshape(heads * latents, shards, depth), 'ctx', spli...  4.73 us
    dot_general x4, matrix products, on_device(): jnp.dot(mixed[head * latents:(head + 1) * latents], cross_v[:, cut], pref...  4.18 us
  transfers between devices with their start and end apart: 3, of which 1 were waited for; matrix products, arithmetic and copies ran while one was open for 4% of the time, Pallas kernels for 0%

commit v1 on v0

--- a/solution.py
+++ b/solution.py
@@ -1,3 +1,4 @@
+import functools
 import math
 import jax
 import jax.numpy as jnp
@@ -8,6 +9,34 @@
 EPS = 1e-05
 NEG = -1e30
 HEADS_AXES = ("tp", "sub")
+
+
+def view_the_members_all(slab_in, axis_key):
+    oldest, arr_now, wide_out = (
+        lax.axis_size(axis_key),
+        lax.axis_index(axis_key),
+        slab_in.shape[0],
+    )
+    shelf = [(p, (p + 1) % oldest) for p in range(oldest)]
+    seen = [(p, (p - 1) % oldest) for p in range(oldest)]
+    shaped = jnp.zeros((*slab_in.shape[:0], oldest * wide_out, *slab_in.shape[1:]), slab_in.dtype)
+    shaped = lax.dynamic_update_slice_in_dim(shaped, slab_in, arr_now * wide_out, axis=0)
+    val2 = res = slab_in
+    local_out = oldest // 2
+    for no in [*range(1, local_out + 1)]:
+        val2 = lax.ppermute(val2, axis_key, shelf)
+        shaped = lax.dynamic_update_slice_in_dim(
+            shaped, val2, (arr_now - no) % oldest * wide_out, axis=0
+        )
+        if no < oldest - local_out:
+            res = lax.ppermute(res, axis_key, seen)
+            shaped = lax.dynamic_update_slice_in_dim(
+                shaped, res, (arr_now + no) % oldest * wide_out, axis=0
+            )
+    return shaped
+
+
+time_corner_up = functools.partial(view_the_members_all, axis_key="ctx")
 
 
 def contract_last(left, right):
@@ -44,7 +73,7 @@
     own = lax.axis_index("ctx")
     mine = lambda array: lax.dynamic_slice_in_dim(array, own * depth, depth, array.ndim - 1)
     whole = lax.all_gather(context, HEADS_AXES, axis=1, tiled=True)
-    all_latents = lax.all_gather(latent_in, "ctx", axis=0, tiled=True).astype(jnp.float32)
+    all_latents = time_corner_up(latent_in).astype(jnp.float32)
     lat_scale = lax.rsqrt(jnp.mean(all_latents * all_latents, axis=1, keepdims=True) + EPS)
     lat_part = mine(all_latents)
     normed_lat = (lat_part * lat_scale * mine(lat_gain)).astype(jnp.bfloat16)

time: 153 us -> 148 us (0.967)
  blocking collectives: 104 us -> 88.4 us
  waiting for transfers between devices: 6.38 us -> 11.4 us
  starting transfers between devices: 8.01 us -> 11.9 us
    all_gather x1 -> x0, blocking collectives: 15.3 us -> none  [on_device(): lax.all_gather(latent_in, 'ctx', axis=0, tiled=True).astype(jnp.float32)]
    ppermute x0 -> x3, waiting for transfers between devices: none -> 5.68 us  [the longest x2 5.67 us: view_the_members_all(): val2 = lax.ppermute(val2, axis_key, shelf)]
    ppermute x0 -> x3, starting transfers between devices: none -> 5.11 us  [the longest x2 3.03 us: view_the_members_all(): val2 = lax.ppermute(val2, axis_key, shelf)]
  transfers between devices with their start and end apart: 3 -> 6, of which waited for: 1 -> 2; matrix products, arithmetic and copies ran while one was open for 4% -> 5% of each run, Pallas kernels for 0% -> 0%
where the time goes in v1:
time: 148 us
  blocking collectives  88.4 us (60%)
  between operations  15 us (10%)
  starting transfers between devices  11.9 us (8%)
  waiting for transfers between devices  11.4 us (8%)
  matrix products  8.52 us (6%)
  local copies, waits for them, and re-layouts  7.2 us (5%)
  other arithmetic  5.33 us (4%)
    all_gather x5, blocking collectives, summed_over(): everything = lax.all_gather(partial.astype(jnp.bfloat16), axis)  53.1 us
    all_gather x1, blocking collectives, on_device(): absorbed = lax.all_gather(absorbed, 'ctx', axis=1, tiled=True)  15.6 us
    all_gather x1, blocking collectives, on_device(): stats = lax.all_gather(jnp.concatenate([top, total], axis=1), 'ctx')  11.3 us
    unnamed x1, blocking collectives  8.34 us
    ppermute x2, waiting for transfers between devices, view_the_members_all(): val2 = lax.ppermute(val2, axis_key, shelf)  5.67 us
    all_to_all x1, waiting for transfers between devices, on_device(): lax.all_to_all(result.reshape(shards, rows, depth), 'ctx', split_axis=0,...  5.66 us
    dot_general x4, matrix products, on_device(): jnp.dot(mixed[head * latents:(head + 1) * latents], cross_v[:, cut], pref...  4.18 us
    all_to_all x1, starting transfers between devices, on_device(): lax.all_to_all(mixed.reshape(heads * latents, shards, depth), 'ctx', spli...  3.47 us
  transfers between devices with their start and end apart: 6, of which 2 were waited for; matrix products, arithmetic and copies ran while one was open for 5% of the time, Pallas kernels for 0%

profile of v1, /device:TPU:0, one launch (start us, length us, event | category | flops | bytes accessed | tf_op | source)
XLA Modules:
  0.0 147.6 jit_solution(12783981143984140093)
XLA Ops:
  6.5 3.0 %collective-permute-start = (bf16[8,2048]{1,0:T(8,128)(2,1)}, bf16[8,2048]{1,0:T(8,128)(2,1)S(1)}, u32[]{:S(2)}, u32[]{:S(2)}) collective-permute-start(bf16[8,2048]{1,0:T(8,128)(2,1)} %param.15), channel_id=1, source_target_pairs={{0,4},{4,8},{8,12},{12,0},{1,5},{5,9},{9,13},{13,1},{2,6},{6,10},{... | collective-permute-start | bytes 98312 | tf_op jit(solution)/shard_map/ppermute | solution.py:27
  9.6 2.1 %collective-permute-start.1 = (bf16[8,2048]{1,0:T(8,128)(2,1)}, bf16[8,2048]{1,0:T(8,128)(2,1)S(1)}, u32[]{:S(2)}, u32[]{:S(2)}) collective-permute-start(bf16[8,2048]{1,0:T(8,128)(2,1)} %param.15), channel_id=1, source_target_pairs={{0,12},{4,0},{8,4},{12,8},{1,13},{5,1},{9,5},{13,9},{2,14},{6,2},{... | collective-permute-start | bytes 98312 | tf_op jit(solution)/shard_map/ppermute | solution.py:32
  12.4 0.8 constant_dynamic-update-slice_fusion.3
  13.9 0.8 broadcast_multiply_fusion
  15.5 5.7 %collective-permute-done.2 = bf16[8,2048]{1,0:T(8,128)(2,1)S(1)} collective-permute-done((bf16[8,2048]{1,0:T(8,128)(2,1)S(1)}, bf16[8,2048]{1,0:T(8,128)(2,1)S(1)}, u32[]{:S(2)}, u32[]{:S(2)}) %collective-permute-start.2) | collective-permute-done | bytes 32800 | tf_op jit(solution)/shard_map/ppermute | solution.py:27
  21.5 13.4 %all-gather = bf16[128,512]{1,0:T(8,128)(2,1)S(1)} all-gather(bf16[32,512]{1,0:T(8,128)(2,1)S(1)} %convolution_convert_fusion.4), channel_id=2, replica_groups=mesh['grp'=2,'ctx'=4,'tp'=2,'sub'=2] {'ctx'}, dimensions={0}, use_global_device_ids=true | all-gather | bytes 163840 | tf_op jit(solution)/shard_map/all_gather | solution.py:49
  35.6 15.6 %all_gather.48 = bf16[128,2048]{1,0:T(8,128)(2,1)S(1)} all-gather(bf16[128,512]{1,0:T(8,128)(2,1)S(1)} %fusion.14), channel_id=1, replica_groups=mesh['grp'=2,'ctx'=4,'tp'=2,'sub'=2] {'ctx'}, dimensions={1}, use_global_device_ids=true | all-gather | bytes 655360 | tf_op jit(solution)/shard_map/all_gather | solution.py:88
  51.2 1.9 %multiply_reduce_fusion = f32[384]{0:T(512)S(1)} fusion(bf16[384,2048]{1,0:T(8,128)(2,1)} %all-gather.8.cloned.1.call-done), kind=kLoop, calls=%fused_computation | loop fusion | flops 2358912 | bytes 1574400 | tf_op jit(solution)/shard_map/reduce_sum | solution.py:90
  54.9 0.9 copy.17
  55.8 3.5 %all-to-all-start = ((bf16[1,128,4,512]{3,1,0,2:T(8,128)(2,1)}), bf16[1,128,4,512]{3,1,0,2:T(8,128)(2,1)S(1)}, u32[]{:S(2)}, u32[]{:S(2)}) async-start(bf16[1,128,4,512]{3,1,0,2:T(8,128)(2,1)} %copy.17), calls=%async_computation | async-start | bytes 1048576 | tf_op jit(solution)/shard_map/all_to_all | solution.py:103
  59.2 0.8 dynamic_slice.19
  60.0 1.7 %copy.18 = bf16[512,3,512]{0,2,1:T(8,128)(2,1)S(1)} copy(bf16[512,3,512]{2,0,1:T(8,128)(2,1)} %param.24) | data formatting | bytes 3145728 | tf_op args[11]
  63.0 11.3 %all-gather.1 = f32[512,2]{0,1:T(2,128)S(1)} all-gather(f32[128,2]{0,1:T(2,128)S(1)} %pad_maximum_fusion.1), channel_id=3, replica_groups=mesh['grp'=2,'ctx'=4,'tp'=2,'sub'=2] {'ctx'}, dimensions={0}, use_global_device_ids=true | all-gather | bytes 5120 | tf_op jit(solution)/shard_map/all_gather | solution.py:106
  74.7 1.0 fusion.10
  75.8 1.0 fusion.11
  76.8 1.0 fusion.12
  77.9 1.0 fusion.9
  78.9 13.4 %all_gather.52 = bf16[4,32,512]{2,1,0:T(8,128)(2,1)S(1)} all-gather(bf16[1,32,512]{2,1,0:T(8,128)(2,1)S(1)} %pad_maximum_fusion), channel_id=1, replica_groups=mesh['grp'=2,'ctx'=4,'tp'=2,'sub'=2] {'ctx'}, dimensions={0}, use_global_device_ids=true | all-gather | bytes 163840 | tf_op jit(solution)/shard_map/all_gather | solution.py:49
  92.6 5.4 %all-gather.2 = bf16[128,512]{1,0:T(8,128)(2,1)S(1)} all-gather(bf16[32,512]{1,0:T(8,128)(2,1)S(1)} %convolution_convert_fusion.3), channel_id=4, replica_groups=mesh['grp'=2,'ctx'=4,'tp'=2,'sub'=2] {'tp','sub'}, dimensions={0}, use_global_device_ids=true | all-gather | bytes 163840 | tf_op jit(solution)/shard_map/all_gather | solution.py:49
  98.8 15.4 %all-gather.3 = bf16[128,1536]{1,0:T(8,128)(2,1)S(1)} all-gather(bf16[32,1536]{1,0:T(8,128)(2,1)S(1)} %convolution_convert_fusion.1), channel_id=5, replica_groups=mesh['grp'=2,'ctx'=4,'tp'=2,'sub'=2] {'ctx'}, dimensions={0}, use_global_device_ids=true | all-gather | bytes 491520 | tf_op jit(solution)/shard_map/all_gather | solution.py:49
  114.7 8.3 %all-reduce = f32[128]{0:T(128)S(1)} all-reduce(f32[128]{0:T(128)S(1)} %dynamic-update-slice), channel_id=6, replica_groups=mesh['grp'=2,'ctx'=4,'tp'=2,'sub'=2] {'ctx'}, use_global_device_ids=true, to_apply=%add | all-reduce | flops 128 | bytes 1024
  125.1 5.4 %all-gather.5 = bf16[128,512]{1,0:T(8,128)(2,1)S(1)} all-gather(bf16[32,512]{1,0:T(8,128)(2,1)S(1)} %convolution_convert_fusion.2), channel_id=7, replica_groups=mesh['grp'=2,'ctx'=4,'tp'=2,'sub'=2] {'tp','sub'}, dimensions={0}, use_global_device_ids=true | all-gather | bytes 163840 | tf_op jit(solution)/shard_map/all_gather | solution.py:49
  131.2 3.3 %all-to-all-start.1 = ((bf16[4,8,1,512]{3,1,2,0:T(8,128)(2,1)}), bf16[4,8,1,512]{3,1,2,0:T(8,128)(2,1)S(1)}, u32[]{:S(2)}, u32[]{:S(2)}) async-start(bf16[4,8,1,512]{3,1,2,0:T(8,128)(2,1)} %fusion.31), calls=%async_computation.1 | async-start | bytes 65536 | tf_op jit(solution)/shard_map/all_to_all | solution.py:148
  134.5 5.7 %all-to-all-done.1 = bf16[4,8,1,512]{3,1,2,0:T(8,128)(2,1)S(1)} async-done(((bf16[4,8,1,512]{3,1,2,0:T(8,128)(2,1)}), bf16[4,8,1,512]{3,1,2,0:T(8,128)(2,1)S(1)}, u32[]{:S(2)}, u32[]{:S(2)}) %all-to-all-start.1) | async-done | bytes 32800 | tf_op jit(solution)/shard_map/all_to_all | solution.py:148
  (80 shorter events, 10.1 us)
Async XLA Ops:
  6.5 14.8 %copy-start = (bf16[512,512]{1,0:T(8,128)(2,1)S(1)}, bf16[512,512]{1,0:T(8,128)(2,1)}, u32[]{:S(2)}) copy-start(bf16[512,512]{1,0:T(8,128)(2,1)} %param.20) | copy-start | bytes 1572868
  6.5 28.4 %copy-start.4 = (bf16[512,512]{1,0:T(8,128)(2,1)S(1)}, bf16[512,512]{1,0:T(8,128)(2,1)}, u32[]{:S(2)}) copy-start(bf16[512,512]{1,0:T(8,128)(2,1)} %param.21) | copy-start | bytes 1572868
  6.5 44.7 %all-gather.8.cloned.1.call-start = ((), (), s32[]{:S(2)}) async-start(), calls=%async_computation.2 | async-start | bytes 1966080 | tf_op jit(solution)/shard_map/all_gather | solution.py:75
  6.5 8.9 %collective-permute-start = (bf16[8,2048]{1,0:T(8,128)(2,1)}, bf16[8,2048]{1,0:T(8,128)(2,1)S(1)}, u32[]{:S(2)}, u32[]{:S(2)}) collective-permute-start(bf16[8,2048]{1,0:T(8,128)(2,1)} %param.15), channel_id=1, source_target_pairs={{0,4},{4,8},{8,12},{12,0},{1,5},{5,9},{9,13},{13,1},{2,6},{6,10},{... | collective-permute-start | bytes 98312 | tf_op jit(solution)/shard_map/ppermute | solution.py:27
  9.6 5.9 %collective-permute-start.1 = (bf16[8,2048]{1,0:T(8,128)(2,1)}, bf16[8,2048]{1,0:T(8,128)(2,1)S(1)}, u32[]{:S(2)}, u32[]{:S(2)}) collective-permute-start(bf16[8,2048]{1,0:T(8,128)(2,1)} %param.15), channel_id=1, source_target_pairs={{0,12},{4,0},{8,4},{12,8},{1,13},{5,1},{9,5},{13,9},{2,14},{6,2},{... | collective-permute-start | bytes 98312 | tf_op jit(solution)/shard_map/ppermute | solution.py:32
  15.4 5.7 %collective-permute-start.2 = (bf16[8,2048]{1,0:T(8,128)(2,1)S(1)}, bf16[8,2048]{1,0:T(8,128)(2,1)S(1)}, u32[]{:S(2)}, u32[]{:S(2)}) collective-permute-start(bf16[8,2048]{1,0:T(8,128)(2,1)S(1)} %collective-permute-done), channel_id=1, source_target_pairs={{0,4},{4,8},{8,12},{12,0},{1,5},{5,9},{9,13},{13,1},{2,6},{6,10},{... | collective-permute-start | bytes 98312 | tf_op jit(solution)/shard_map/ppermute | solution.py:27
  51.2 1.9 %copy-start.1 = (bf16[384,2048]{1,0:T(8,128)(2,1)S(1)}, bf16[384,2048]{1,0:T(8,128)(2,1)}, u32[]{:S(2)}) copy-start(bf16[384,2048]{1,0:T(8,128)(2,1)} %all-gather.8.cloned.1.call-done) | copy-start | bytes 4718596
  55.8 18.7 %all-to-all-start = ((bf16[1,128,4,512]{3,1,0,2:T(8,128)(2,1)}), bf16[1,128,4,512]{3,1,0,2:T(8,128)(2,1)S(1)}, u32[]{:S(2)}, u32[]{:S(2)}) async-start(bf16[1,128,4,512]{3,1,0,2:T(8,128)(2,1)} %copy.17), calls=%async_computation | async-start | bytes 1048576 | tf_op jit(solution)/shard_map/all_to_all | solution.py:103
  60.0 1.8 %copy-start.5 = (u32[32]{0:T(128)S(1)}, u32[32]{0:T(128)}, u32[]{:S(2)}) copy-start(u32[32]{0:T(128)} %constant.76) | copy-start | bytes 388
  61.8 30.6 %copy-start.2 = (bf16[512,512]{1,0:T(8,128)(2,1)S(1)}, bf16[512,512]{1,0:T(8,128)(2,1)}, u32[]{:S(2)}) copy-start(bf16[512,512]{1,0:T(8,128)(2,1)} %param.23) | copy-start | bytes 1572868
  98.7 26.1 %copy-start.3 = (bf16[512,512]{1,0:T(8,128)(2,1)S(1)}, bf16[512,512]{1,0:T(8,128)(2,1)}, u32[]{:S(2)}) copy-start(bf16[512,512]{1,0:T(8,128)(2,1)} %param.25) | copy-start | bytes 1572868
  131.2 8.9 %all-to-all-start.1 = ((bf16[4,8,1,512]{3,1,2,0:T(8,128)(2,1)}), bf16[4,8,1,512]{3,1,2,0:T(8,128)(2,1)S(1)}, u32[]{:S(2)}, u32[]{:S(2)}) async-start(bf16[4,8,1,512]{3,1,2,0:T(8,128)(2,1)} %fusion.31), calls=%async_computation.1 | async-start | bytes 65536 | tf_op jit(solution)/shard_map/all_to_all | solution.py:148
Sparse Core Ops, SparseCore 0:
  11.8 19.4 all-gather.7
